TPU v7x, 32 devices: a whole 2x2x4 slice. The times are simulated.
32 devices in a mesh: groups: 2 (over y), row: 8 (over z, x), col: 2 (over core).
Axes of the slice: x: 2, y: 2, z: 4, core: 2. Of those that a mesh axis runs over, the one named last changes fastest.
Arguments:
- gram_old: bfloat16 [28672, 14336], P(('groups', 'row'), 'col'), parts along dimension 0, may hold values from -10 to 256, as said below
- activations: bfloat16 [256, 14336], P('groups', 'row'), parts along dimension 0, may hold values from -0.5 to 0.5
- weights: float32 [14336, 512], P('row', ('groups', 'col')), parts along dimension 1, may hold values from -6 to 6
- block_mask: int32 [112, 4], P(None, 'groups'), parts along dimension 1, may hold values 0 or 1
Outputs:
- pruned: float32 [14336, 512], P('row', ('groups', 'col')), parts along dimension 1
There are 2 independent parts, one for each index of `groups`. A program takes and returns all parts, laid end to end along the dimension named above; each array names one. Nothing has to cross between parts.
Inputs may be any that keep to these rules, and one draw needn't show every extreme that they name: `gram_old`: symmetric and positive definite.
All inputs are finite; a program needn't handle non-finite values.
Results may differ from a plain program's by a relative error of at most 0.00076.
Values may be sent and summed in bfloat16 or wider, within the bound.
A program may use at most 128 MiB of HBM per device.

v0:
```python
import jax
import jax.numpy as jnp
from jax import lax
from jax.sharding import PartitionSpec as P

K = 14336
BLK = 128


damping_ratio = 0.3
epsilon = 1e-06


def partner(value, axis, distance):
    return lax.ppermute(value, axis, [(i, i ^ 1 << distance) for i in range(lax.axis_size(axis))])


def expand_local(block_mask, row_offset, row_count, col_offset, col_count):
    row_ids = (row_offset + jnp.arange(row_count, dtype=jnp.int32)) // BLK
    col_ids = (col_offset + jnp.arange(col_count, dtype=jnp.int32)) // BLK
    pick_rows = (
        row_ids[:, None] == jnp.arange(block_mask.shape[0], dtype=jnp.int32)[None, :]
    ).astype(jnp.float32)
    pick_cols = (
        col_ids[:, None] == jnp.arange(block_mask.shape[1], dtype=jnp.int32)[None, :]
    ).astype(jnp.float32)
    partial_rows = jnp.dot(
        pick_rows, block_mask.astype(jnp.float32), precision=lax.Precision.HIGHEST
    )
    return jnp.dot(partial_rows, pick_cols.T, precision=lax.Precision.HIGHEST)


def per_device(gram_old, activations, weights, block_mask):
    row_block = gram_old.shape[0]
    half_width = gram_old.shape[1]
    width_cols = weights.shape[1]
    row_index = lax.axis_index("row")
    col_index = lax.axis_index("col")
    row_offset = row_index * row_block
    half_offset = col_index * half_width
    gathered = lax.all_gather(activations, "row", axis=1, tiled=True)
    half_acts = lax.dynamic_slice_in_dim(gathered, half_offset, half_width, 1)
    gram_update = lax.dot_general(
        activations, half_acts, (((0,), (0,)), ((), ())), preferred_element_type=jnp.float32
    )
    gram_new = (gram_old.astype(jnp.float32) + gram_update).astype(jnp.bfloat16)
    diag_column = row_offset + jnp.arange(row_block, dtype=jnp.int32) - half_offset
    on_diagonal = jnp.arange(half_width, dtype=jnp.int32)[None, :] == diag_column[:, None]
    trace_part = jnp.sum(jnp.where(on_diagonal, gram_new.astype(jnp.float32), 0.0))
    trace_total = lax.psum(trace_part, ("row", "col"))
    mask_local = expand_local(block_mask, row_offset, row_block, col_index * width_cols, width_cols)

    def apply_gram(panel):
        column_panel = lax.all_gather(panel.astype(jnp.bfloat16), "row", axis=0, tiled=True)
        own_half = lax.dynamic_slice_in_dim(column_panel, half_offset, half_width, 0)
        partner_need = lax.dynamic_slice_in_dim(
            column_panel, (1 - col_index) * half_width, half_width, 0
        )
        partner_half = partner(partner_need, "col", 0)
        own_part = jnp.dot(gram_new, own_half, preferred_element_type=jnp.float32)
        partner_part = jnp.dot(gram_new, partner_half, preferred_element_type=jnp.float32)
        return own_part + partner(partner_part, "col", 0)

    kept_weights = mask_local * weights
    pruned_diff = kept_weights - weights
    grad_first = apply_gram(pruned_diff)
    step_dir = mask_local * grad_first
    curvature = apply_gram(step_dir)
    masked_curve = mask_local * curvature
    local_square = jnp.sum(step_dir * step_dir)
    local_curve = jnp.sum(step_dir * curvature)
    local_curve_square = jnp.sum(masked_curve * masked_curve)
    grad_square, grad_curve, curve_square = lax.psum(
        (local_square, local_curve, local_curve_square), ("row", "col")
    )
    damping = damping_ratio * trace_total / K
    step_first = grad_square / (grad_curve + damping * grad_square + epsilon)
    step_second = (grad_curve + damping * grad_square) / (
        curve_square + 2.0 * damping * grad_curve + damping * damping * grad_square + epsilon
    )
    grad_second = grad_first - step_first * curvature
    return kept_weights - step_first * step_dir - step_second * (mask_local * grad_second)


def solution(mesh):
    placed = (
        P(("groups", "row"), "col"),
        P("groups", "row"),
        P("row", ("groups", "col")),
        P(None, "groups"),
    )
    return jax.shard_map(
        per_device,
        mesh=mesh,
        in_specs=placed,
        out_specs=P("row", ("groups", "col")),
        check_vma=False,
    )
```

profile of v0, /device:TPU:0, one launch (start us, length us, event | category | flops | bytes accessed | tf_op | source)
XLA Modules:
  0.0 342.0 jit_solution(2556524384212306083)
XLA Ops:
  6.6 2.0 fusion.9
  8.6 2.9 subtract_convert_fusion
  11.5 0.0 all-gather.4.cloned.1.call-start
  11.6 0.7 all-gather.4.cloned.1.call-update
  12.3 31.9 %copy.5 = bf16[1792,7168]{0,1:T(8,128)(2,1)} copy(bf16[1792,7168]{1,0:T(8,128)(2,1)} %param.4) | data formatting | bytes 51380224 | tf_op args[0]
  44.3 36.4 %all-gather.6.cloned.1.call-done = bf16[14336,128]{1,0:T(8,128)(2,1)} async-done(((bf16[1792,128]{1,0:T(8,128)(2,1)}), bf16[14336,128]{1,0:T(8,128)(2,1)}) %all-gather.6.cloned.1.call-update) | async-done | bytes 3670032 | tf_op jit(solution)/shard_map/all_gather | solution.py:54
  80.6 1.6 constant_dynamic-slice_fusion.1
  82.2 0.1 collective-permute-start
  82.3 65.5 %all-gather.4.cloned.1.call-done = bf16[128,14336]{1,0:T(8,128)(2,1)} async-done(((bf16[128,1792]{1,0:T(8,128)(2,1)}), bf16[128,14336]{1,0:T(8,128)(2,1)}) %all-gather.4.cloned.1.call-update) | async-done | bytes 3670032 | tf_op jit(solution)/shard_map/all_gather | solution.py:41
  147.8 22.2 %select_reduce_fusion = (f32[]{:T(128)}, bf16[1792,7168]{0,1:T(8,128)(2,1)}) fusion(s32[1792]{0:T(1024)S(1)} %fusion.14, bf16[128,1792]{1,0:T(8,128)(2,1)S(1)} %copy-done.2, bf16[128,14336]{1,0:T(8,128)(2,1)} %all-gather.4.cloned.1.call-done, s32[]{:T(128)S(6)} %select_n.33, bf16[1792,7168]{0,1:T(8,128)(2,1)} %copy.5), kind=kOutput, calls=%fused_computation.2 | convolution fusion | flops 3378249728 | bytes 53681160 | tf_op jit(solution)/shard_map/dot_general | solution.py:43
  170.1 12.5 %fusion.22 = f32[1792,128]{1,0:T(8,128)S(1)} fusion(bf16[1792,7168]{0,1:T(8,128)(2,1)} %get-tuple-element.20, bf16[7168,128]{1,0:T(8,128)(2,1)} %collective-permute-done), kind=kOutput, calls=%fused_computation.42 | convolution fusion | flops 3288334336 | bytes 28442624 | tf_op jit(solution)/shard_map/dot_general | solution.py:61
  182.6 0.1 collective-permute-start.1
  182.6 11.9 %fusion.6 = f32[1792,128]{1,0:T(8,128)S(1)} fusion(bf16[1792,7168]{0,1:T(8,128)(2,1)} %get-tuple-element.20, bf16[14336,128]{1,0:T(8,128)(2,1)S(1)} %copy-done, s32[]{:T(128)S(6)} %select_n.33), kind=kOutput, calls=%fused_computation.7 | convolution fusion | flops 3288334336 | bytes 28442628 | tf_op jit(solution)/shard_map/dot_general | solution.py:60
  194.5 1.1 fusion.21
  195.6 65.1 %all-gather.8.cloned.1.call-done = bf16[14336,128]{1,0:T(8,128)(2,1)} async-done(((bf16[1792,128]{1,0:T(8,128)(2,1)}), bf16[14336,128]{1,0:T(8,128)(2,1)}) %all-gather.8.cloned.1.call-update) | async-done | bytes 3670032 | tf_op jit(solution)/shard_map/all_gather | solution.py:54
  260.8 1.6 constant_dynamic-slice_fusion
  262.4 0.1 collective-permute-start.2
  262.5 3.8 %collective-permute-done.2 = bf16[7168,128]{1,0:T(8,128)(2,1)S(1)} collective-permute-done((bf16[7168,128]{1,0:T(8,128)(2,1)S(1)}, bf16[7168,128]{1,0:T(8,128)(2,1)S(1)}, u32[]{:S(2)}, u32[]{:S(2)}) %collective-permute-start.2) | collective-permute-done | bytes 1835040 | tf_op jit(solution)/shard_map/ppermute | solution.py:15
  266.3 11.9 %fusion.23 = f32[1792,128]{1,0:T(8,128)S(1)} fusion(bf16[1792,7168]{0,1:T(8,128)(2,1)} %get-tuple-element.20, bf16[7168,128]{1,0:T(8,128)(2,1)S(1)} %collective-permute-done.2), kind=kOutput, calls=%fused_computation.43 | convolution fusion | flops 3288334336 | bytes 28442624 | tf_op jit(solution)/shard_map/dot_general | solution.py:61
  278.1 0.2 collective-permute-start.3
  278.3 2.3 collective-permute-done.3
  280.7 13.7 %multiply_reduce_fusion = (f32[]{:T(128)}, f32[]{:T(128)}, f32[]{:T(128)}, f32[1792,128]{1,0:T(8,128)}) fusion(f32[1792,128]{1,0:T(8,128)S(1)} %get-tuple-element.17, f32[1792,128]{1,0:T(8,128)S(1)} %get-tuple-element.13, f32[1792,128]{1,0:T(8,128)S(1)} %collective-permute-done.3, bf16[1792,7168]{0,1:T(8,128)(2,1)} %get-tuple-element.20, ...), kind=kOutput, calls=%fused_computation.11 | convolution fusion | flops 3290169344 | bytes 31195152 | tf_op jit(solution)/shard_map/dot_general | solution.py:60
  294.4 31.9 %all-reduce = (f32[]{:T(128)}, f32[]{:T(128)}, f32[]{:T(128)}, f32[]{:T(128)}) all-reduce(f32[]{:T(128)} %get-tuple-element.6, f32[]{:T(128)} %get-tuple-element.19, f32[]{:T(128)} %get-tuple-element.7, f32[]{:T(128)} %get-tuple-element.5), channel_id=1, replica_groups=mesh['groups'=2,'row'=8,'col'=2] {'row','col'}, use_global_device_ids=true, to_apply=%region_3.4 | all-reduce | flops 4 | bytes 32 | tf_op jit(solution)/shard_map/psum | solution.py:73
  332.9 2.6 multiply_subtract_fusion
  (15 shorter events, 0.1 us)
Async XLA Ops:
  6.5 74.1 %all-gather.6.cloned.1.call-start = ((), (), s32[]{:S(2)}) async-start(), calls=%async_computation.1 | async-start | bytes 4128768 | tf_op jit(solution)/shard_map/all_gather | solution.py:54
  11.5 136.3 %all-gather.4.cloned.1.call-start = ((), (), s32[]{:S(2)}) async-start(), calls=%async_computation | async-start | bytes 4128768 | tf_op jit(solution)/shard_map/all_gather | solution.py:41
  12.3 248.5 %all-gather.8.cloned.1.call-start = ((), (), s32[]{:S(2)}) async-start(), calls=%async_computation.2 | async-start | bytes 4128768 | tf_op jit(solution)/shard_map/all_gather | solution.py:54
  44.2 103.6 %copy-start.2 = (bf16[128,1792]{1,0:T(8,128)(2,1)S(1)}, bf16[128,1792]{1,0:T(8,128)(2,1)}, u32[]{:S(2)}) copy-start(bf16[128,1792]{1,0:T(8,128)(2,1)} %param.5) | copy-start | bytes 1376260
  82.2 87.8 %collective-permute-start = (bf16[7168,128]{1,0:T(8,128)(2,1)S(1)}, bf16[7168,128]{1,0:T(8,128)(2,1)}, u32[]{:S(2)}, u32[]{:S(2)}) collective-permute-start(bf16[7168,128]{1,0:T(8,128)(2,1)S(1)} %constant_dynamic-slice_fusion.1), channel_id=1, source_target_pairs={{0,1},{1,0},{2,3},{3,2},{4,5},{5,4},{6,7},{7,6},{8,9},{9,8},{10,11... | collective-permute-start | bytes 5505032 | tf_op jit(solution)/shard_map/ppermute | solution.py:15
  170.1 12.6 %copy-start = (bf16[14336,128]{1,0:T(8,128)(2,1)S(1)}, bf16[14336,128]{1,0:T(8,128)(2,1)}, u32[]{:S(2)}) copy-start(bf16[14336,128]{1,0:T(8,128)(2,1)} %all-gather.6.cloned.1.call-done) | copy-start | bytes 11010052
  182.6 12.0 %collective-permute-start.1 = (f32[1792,128]{1,0:T(8,128)S(1)}, f32[1792,128]{1,0:T(8,128)S(1)}, u32[]{:S(2)}, u32[]{:S(2)}) collective-permute-start(f32[1792,128]{1,0:T(8,128)S(1)} %fusion.22), channel_id=1, source_target_pairs={{0,1},{1,0},{2,3},{3,2},{4,5},{5,4},{6,7},{7,6},{8,9},{9,8},{10,11... | collective-permute-start | bytes 2752520 | tf_op jit(solution)/shard_map/ppermute | solution.py:15
  262.4 18.3 %copy-start.1 = (bf16[14336,128]{1,0:T(8,128)(2,1)S(1)}, bf16[14336,128]{1,0:T(8,128)(2,1)}, u32[]{:S(2)}) copy-start(bf16[14336,128]{1,0:T(8,128)(2,1)} %all-gather.8.cloned.1.call-done) | copy-start | bytes 11010052
  262.4 3.9 %collective-permute-start.2 = (bf16[7168,128]{1,0:T(8,128)(2,1)S(1)}, bf16[7168,128]{1,0:T(8,128)(2,1)S(1)}, u32[]{:S(2)}, u32[]{:S(2)}) collective-permute-start(bf16[7168,128]{1,0:T(8,128)(2,1)S(1)} %constant_dynamic-slice_fusion), channel_id=1, source_target_pairs={{0,1},{1,0},{2,3},{3,2},{4,5},{5,4},{6,7},{7,6},{8,9},{9,8},{10,11... | collective-permute-start | bytes 5505032 | tf_op jit(solution)/shard_map/ppermute | solution.py:15
  278.1 2.5 collective-permute-start.3
Sparse Core Ops, SparseCore 0:
  11.6 68.9 all-gather.5
  82.8 64.9 all-gather.3
  195.8 64.9 all-gather.7
where the time goes:
time: 343 us; the launch traced here: 342 us
  waiting for transfers between devices  174 us (51%)
  matrix products  77.1 us (22%)
  local copies, waits for them, and re-layouts  35.2 us (10%)
  blocking collectives  31.9 us (9%)
  between operations  19.7 us (6%)
  other arithmetic  3.71 us (1%)
    all_gather x2, waiting for transfers between devices, apply_gram(): lax.all_gather(panel.astype(jnp.bfloat16), 'row', axis=0, tiled=True)  101 us
    all_gather x1, waiting for transfers between devices, per_device(): gathered = lax.all_gather(activations, 'row', axis=1, tiled=True)  65.5 us
    psum x1, blocking collectives, per_device(): lax.psum((local_square, local_curve, local_curve_square), ('row', 'col'))  31.9 us
    unnamed x7, local copies, waits for them, and re-layouts  31.9 us
    dot_general x2, matrix products, apply_gram(): own_part = jnp.dot(gram_new, own_half, preferred_element_type=jnp.float32)  25.6 us
    dot_general x2, matrix products, apply_gram(): jnp.dot(gram_new, partner_half, preferred_element_type=jnp.float32)  24.4 us
    dot_general x1, matrix products, per_device(): lax.dot_general(activations, half_acts, (((0,), (0,)), ((), ())), preferr...  22.2 us
  transfers between devices with their start and end apart: 7, of which 5 were waited for; matrix products, arithmetic and copies ran while one was open for 20% of the time, Pallas kernels for 0%

commit v1 on v0

--- a/solution.py
+++ b/solution.py
@@ -30,6 +30,15 @@
     return jnp.dot(partial_rows, pick_cols.T, precision=lax.Precision.HIGHEST)
 
 
+def update_product(activations, inner):
+    high = inner.astype(jnp.bfloat16)
+    low = (inner - high.astype(jnp.float32)).astype(jnp.bfloat16)
+    contract = (((0,), (0,)), ((), ()))
+    return lax.dot_general(
+        activations, high, contract, preferred_element_type=jnp.float32
+    ) + lax.dot_general(activations, low, contract, preferred_element_type=jnp.float32)
+
+
 def per_device(gram_old, activations, weights, block_mask):
     row_block = gram_old.shape[0]
     half_width = gram_old.shape[1]
@@ -38,28 +47,28 @@
     col_index = lax.axis_index("col")
     row_offset = row_index * row_block
     half_offset = col_index * half_width
-    gathered = lax.all_gather(activations, "row", axis=1, tiled=True)
-    half_acts = lax.dynamic_slice_in_dim(gathered, half_offset, half_width, 1)
-    gram_update = lax.dot_general(
-        activations, half_acts, (((0,), (0,)), ((), ())), preferred_element_type=jnp.float32
-    )
-    gram_new = (gram_old.astype(jnp.float32) + gram_update).astype(jnp.bfloat16)
     diag_column = row_offset + jnp.arange(row_block, dtype=jnp.int32) - half_offset
     on_diagonal = jnp.arange(half_width, dtype=jnp.int32)[None, :] == diag_column[:, None]
-    trace_part = jnp.sum(jnp.where(on_diagonal, gram_new.astype(jnp.float32), 0.0))
-    trace_total = lax.psum(trace_part, ("row", "col"))
+    trace_part = jnp.sum(jnp.where(on_diagonal, gram_old.astype(jnp.float32), 0.0))
+    acts_wide = activations.astype(jnp.float32)
+    trace_part = trace_part + jnp.sum(acts_wide * acts_wide) / lax.axis_size("col")
     mask_local = expand_local(block_mask, row_offset, row_block, col_index * width_cols, width_cols)
 
     def apply_gram(panel):
-        column_panel = lax.all_gather(panel.astype(jnp.bfloat16), "row", axis=0, tiled=True)
+        panel_low = panel.astype(jnp.bfloat16)
+        inner = lax.psum(
+            jnp.dot(activations, panel_low, preferred_element_type=jnp.float32), "row"
+        )
+        low_rank = update_product(activations, inner)
+        column_panel = lax.all_gather(panel_low, "row", axis=0, tiled=True)
         own_half = lax.dynamic_slice_in_dim(column_panel, half_offset, half_width, 0)
         partner_need = lax.dynamic_slice_in_dim(
             column_panel, (1 - col_index) * half_width, half_width, 0
         )
         partner_half = partner(partner_need, "col", 0)
-        own_part = jnp.dot(gram_new, own_half, preferred_element_type=jnp.float32)
-        partner_part = jnp.dot(gram_new, partner_half, preferred_element_type=jnp.float32)
-        return own_part + partner(partner_part, "col", 0)
+        own_part = jnp.dot(gram_old, own_half, preferred_element_type=jnp.float32)
+        partner_part = jnp.dot(gram_old, partner_half, preferred_element_type=jnp.float32)
+        return own_part + partner(partner_part, "col", 0) + low_rank
 
     kept_weights = mask_local * weights
     pruned_diff = kept_weights - weights
@@ -70,8 +79,8 @@
     local_square = jnp.sum(step_dir * step_dir)
     local_curve = jnp.sum(step_dir * curvature)
     local_curve_square = jnp.sum(masked_curve * masked_curve)
-    grad_square, grad_curve, curve_square = lax.psum(
-        (local_square, local_curve, local_curve_square), ("row", "col")
+    grad_square, grad_curve, curve_square, trace_total = lax.psum(
+        jnp.stack([local_square, local_curve, local_curve_square, trace_part]), ("row", "col")
     )
     damping = damping_ratio * trace_total / K
     step_first = grad_square / (grad_curve + damping * grad_square + epsilon)

time: 343 us -> 420 us (1.22)
  waiting for transfers between devices: 174 us -> 270 us
  local copies, waits for them, and re-layouts: 35.2 us -> 5.13 us
  other arithmetic: 3.71 us -> 29.6 us
  matrix products: 77.1 us -> 63.5 us
    psum x0 -> x2, waiting for transfers between devices: none -> 134 us  [apply_gram(): lax.psum(jnp.dot(activations, panel_low, preferred_element_type=jnp.float...]
    unnamed x7 -> x12, local copies, waits for them, and re-layouts: 31.9 us -> 0.03 us
    all_gather x3 -> x2, waiting for transfers between devices: 167 us -> 135 us  [apply_gram(): column_panel = lax.all_gather(panel_low, 'row', axis=0, tiled=True)]
    reduce_sum x0 -> x2, other arithmetic: none -> 24.4 us  [the longest x1 23.6 us: per_device(): jnp.sum(jnp.where(on_diagonal, gram_old.astype(jnp.float32), 0.0))]
    dot_general x5 -> x10, matrix products: 72.2 us -> 58.5 us  [the longest x2 25.8 us: apply_gram(): own_part = jnp.dot(gram_old, own_half, preferred_element_type=jnp.float32)]
    ppermute x4, waiting for transfers between devices: 6.11 us -> 0.01 us  [partner(): lax.ppermute(value, axis, [(i, i ^ 1 << distance) for i in range(lax.axis...]
  transfers between devices with their start and end apart: 7 -> 8, of which waited for: 5 -> 4; matrix products, arithmetic and copies ran while one was open for 20% -> 10% of each run, Pallas kernels for 0% -> 0%
where the time goes in v1:
time: 420 us
  waiting for transfers between devices  270 us (64%)
  matrix products  63.5 us (15%)
  blocking collectives  30.3 us (7%)
  other arithmetic  29.6 us (7%)
  between operations  20.8 us (5%)
  local copies, waits for them, and re-layouts  5.13 us (1%)
    all_gather x2, waiting for transfers between devices, apply_gram(): column_panel = lax.all_gather(panel_low, 'row', axis=0, tiled=True)  135 us
    psum x2, waiting for transfers between devices, apply_gram(): lax.psum(jnp.dot(activations, panel_low, preferred_element_type=jnp.float...  134 us
    psum x1, blocking collectives, per_device(): lax.psum(jnp.stack([local_square, local_curve, local_curve_square, trace_...  30.3 us
    dot_general x2, matrix products, apply_gram(): own_part = jnp.dot(gram_old, own_half, preferred_element_type=jnp.float32)  25.8 us
    dot_general x2, matrix products, apply_gram(): jnp.dot(gram_old, partner_half, preferred_element_type=jnp.float32)  25.3 us
    reduce_sum x1, other arithmetic, per_device(): jnp.sum(jnp.where(on_diagonal, gram_old.astype(jnp.float32), 0.0))  23.6 us
  transfers between devices with their start and end apart: 8, of which 4 were waited for; matrix products, arithmetic and copies ran while one was open for 10% of the time, Pallas kernels for 0%

profile of v1, /device:TPU:0, one launch (start us, length us, event | category | flops | bytes accessed | tf_op | source)
XLA Modules:
  0.0 419.9 jit_solution(6358814029816759565)
XLA Ops:
  6.6 2.0 fusion.4
  8.6 2.9 subtract_convert_fusion
  11.6 69.0 %all-gather.3.cloned.1.call-done = bf16[14336,128]{1,0:T(8,128)(2,1)} async-done(((bf16[1792,128]{1,0:T(8,128)(2,1)}), bf16[14336,128]{1,0:T(8,128)(2,1)}) %all-gather.3.cloned.1.call-update) | async-done | bytes 3670032 | tf_op jit(solution)/shard_map/all_gather | solution.py:63
  80.7 2.9 constant_dynamic-slice_fusion.1
  83.5 0.9 convolution_bitcast_fusion.5
  84.6 68.2 %all-reduce.3.cloned.1.call-done = f32[128,128]{0,1:T(8,128)} async-done(((f32[128,128]{0,1:T(8,128)}), f32[128,128]{0,1:T(8,128)}) %all-reduce.3.cloned.1.call-update) | async-done | bytes 65552 | tf_op jit(solution)/shard_map/psum | solution.py:59
  152.8 1.2 fusion.12
  154.0 12.5 %convolution_bitcast_fusion.2 = f32[1792,128]{1,0:T(8,128)S(1)} fusion(bf16[1792,7168]{1,0:T(8,128)(2,1)} %param.4, bf16[7168,128]{1,0:T(8,128)(2,1)} %collective-permute-done), kind=kOutput, calls=%fused_computation.6 | convolution fusion | flops 3288334336 | bytes 28442624 | tf_op jit(solution)/shard_map/dot_general | solution.py:70
  166.5 11.8 %convolution_bitcast_fusion.3 = f32[1792,128]{1,0:T(8,128)S(1)} fusion(bf16[1792,7168]{1,0:T(8,128)(2,1)} %param.4, bf16[14336,128]{1,0:T(8,128)(2,1)S(1)} %copy-done.4, s32[]{:T(128)S(6)} %select_n.32), kind=kOutput, calls=%fused_computation.7 | convolution fusion | flops 3288334336 | bytes 28442628 | tf_op jit(solution)/shard_map/dot_general | solution.py:69
  178.4 1.8 fusion.24
  180.5 66.2 %all-gather.5.cloned.1.call-done = bf16[14336,128]{1,0:T(8,128)(2,1)} async-done(((bf16[1792,128]{1,0:T(8,128)(2,1)}), bf16[14336,128]{1,0:T(8,128)(2,1)}) %all-gather.5.cloned.1.call-update) | async-done | bytes 3670032 | tf_op jit(solution)/shard_map/all_gather | solution.py:63
  246.7 1.6 constant_dynamic-slice_fusion
  248.4 23.6 %select_reduce_fusion = f32[]{:T(128)} fusion(bf16[1792,7168]{1,0:T(8,128)(2,1)} %param.4, s32[1792]{0:T(1024)S(1)} %get-tuple-element.20), kind=kLoop, calls=%fused_computation | loop fusion | flops 51380224 | bytes 25697284 | tf_op jit(solution)/shard_map/reduce_sum | solution.py:52
  272.0 12.8 %convolution_bitcast_fusion = f32[1792,128]{1,0:T(8,128)} fusion(bf16[1792,7168]{1,0:T(8,128)(2,1)} %param.4, bf16[7168,128]{1,0:T(8,128)(2,1)S(1)} %collective-permute-done.2), kind=kOutput, calls=%fused_computation.4 | convolution fusion | flops 3288334336 | bytes 28442624 | tf_op jit(solution)/shard_map/dot_general | solution.py:70
  285.3 1.0 convolution_bitcast_fusion.4
  286.3 0.8 multiply_reduce_fusion
  288.3 66.2 %all-reduce.5.cloned.1.call-done = f32[128,128]{0,1:T(8,128)} async-done(((f32[128,128]{0,1:T(8,128)}), f32[128,128]{0,1:T(8,128)}) %all-reduce.5.cloned.1.call-update) | async-done | bytes 65552 | tf_op jit(solution)/shard_map/psum | solution.py:59
  354.5 1.2 fusion.9
  355.7 1.2 fusion.1
  357.0 14.0 %multiply_reduce_fusion.3 = (f32[]{:T(128)}, f32[]{:T(128)}, f32[]{:T(128)}, f32[1792,128]{1,0:T(8,128)}) fusion(f32[1792,128]{1,0:T(8,128)S(1)} %copy-done.3, f32[1792,128]{1,0:T(8,128)S(1)} %get-tuple-element.16, f32[1792,128]{1,0:T(8,128)S(1)} %fusion.1, f32[1792,128]{1,0:T(8,128)} %collective-permute-done.3, bf16[1792,7168]{1,0:T(8,128)(2,1)} %param.4, ...), kind=kOutput, calls=%fused_computation.19 | convolution fusion | flops 3290398720 | bytes 32112656 | tf_op jit(solution)/shard_map/dot_general | solution.py:69
  371.0 2.0 pad_maximum_fusion
  373.0 30.3 %psum.23 = f32[4]{0:T(128)S(1)} all-reduce(f32[4]{0:T(128)S(1)} %pad_maximum_fusion), channel_id=1, replica_groups=mesh['groups'=2,'row'=8,'col'=2] {'row','col'}, use_global_device_ids=true, to_apply=%region_7.8 | all-reduce | flops 4 | bytes 32 | tf_op jit(solution)/shard_map/psum | solution.py:82
  403.2 0.6 fusion.26
  410.2 3.2 multiply_subtract_fusion
  (30 shorter events, 1.1 us)
Async XLA Ops:
  6.5 74.1 %all-gather.3.cloned.1.call-start = ((), (), s32[]{:S(2)}) async-start(), calls=%async_computation | async-start | bytes 4128768 | tf_op jit(solution)/shard_map/all_gather | solution.py:63
  8.6 74.9 %copy-start = (bf16[128,1792]{1,0:T(8,128)(2,1)S(1)}, bf16[128,1792]{1,0:T(8,128)(2,1)}, u32[]{:S(2)}) copy-start(bf16[128,1792]{1,0:T(8,128)(2,1)} %param.5) | copy-start | bytes 1376260
  11.6 72.0 %copy-start.2 = (bf16[1792,128]{1,0:T(8,128)(2,1)S(1)}, bf16[1792,128]{1,0:T(8,128)(2,1)}, u32[]{:S(2)}) copy-start(bf16[1792,128]{1,0:T(8,128)(2,1)} %get-tuple-element.10) | copy-start | bytes 1376260
  11.6 141.2 %all-reduce.3.cloned.1.call-start = ((), (), s32[]{:S(2)}) async-start(), calls=%async_computation.1 | async-start | bytes 131072 | tf_op jit(solution)/shard_map/psum | solution.py:59
  83.5 70.4 %collective-permute-start = (bf16[7168,128]{1,0:T(8,128)(2,1)}, bf16[7168,128]{1,0:T(8,128)(2,1)}, u32[]{:S(2)}, u32[]{:S(2)}) collective-permute-start(bf16[7168,128]{1,0:T(8,128)(2,1)} %constant_dynamic-slice_fusion.1), channel_id=1, source_target_pairs={{0,1},{1,0},{2,3},{3,2},{4,5},{5,4},{6,7},{7,6},{8,9},{9,8},{10,11... | collective-permute-start | bytes 5505032 | tf_op jit(solution)/shard_map/ppermute | solution.py:15
  84.5 162.2 %all-gather.5.cloned.1.call-start = ((), (), s32[]{:S(2)}) async-start(), calls=%async_computation.2 | async-start | bytes 4128768 | tf_op jit(solution)/shard_map/all_gather | solution.py:63
  153.9 12.6 %copy-start.4 = (bf16[14336,128]{1,0:T(8,128)(2,1)S(1)}, bf16[14336,128]{1,0:T(8,128)(2,1)}, u32[]{:S(2)}) copy-start(bf16[14336,128]{1,0:T(8,128)(2,1)} %all-gather.3.cloned.1.call-done) | copy-start | bytes 11010052
  166.4 11.9 %copy-start.5 = (f32[128,128]{0,1:T(8,128)S(1)}, f32[128,128]{0,1:T(8,128)}, u32[]{:S(2)}) copy-start(f32[128,128]{0,1:T(8,128)} %all-reduce.3.cloned.1.call-done) | copy-start | bytes 196612
  166.5 11.9 %collective-permute-start.1 = (f32[1792,128]{1,0:T(8,128)S(1)}, f32[1792,128]{1,0:T(8,128)S(1)}, u32[]{:S(2)}, u32[]{:S(2)}) collective-permute-start(f32[1792,128]{1,0:T(8,128)S(1)} %convolution_bitcast_fusion.2), channel_id=1, source_target_pairs={{0,1},{1,0},{2,3},{3,2},{4,5},{5,4},{6,7},{7,6},{8,9},{9,8},{10,11... | collective-permute-start | bytes 2752520 | tf_op jit(solution)/shard_map/ppermute | solution.py:15
  180.2 174.2 %all-reduce.5.cloned.1.call-start = ((), (), s32[]{:S(2)}) async-start(), calls=%async_computation.3 | async-start | bytes 131072 | tf_op jit(solution)/shard_map/psum | solution.py:59
  248.3 23.7 %collective-permute-start.2 = (bf16[7168,128]{1,0:T(8,128)(2,1)S(1)}, bf16[7168,128]{1,0:T(8,128)(2,1)S(1)}, u32[]{:S(2)}, u32[]{:S(2)}) collective-permute-start(bf16[7168,128]{1,0:T(8,128)(2,1)S(1)} %constant_dynamic-slice_fusion), channel_id=1, source_target_pairs={{0,1},{1,0},{2,3},{3,2},{4,5},{5,4},{6,7},{7,6},{8,9},{9,8},{10,11... | collective-permute-start | bytes 5505032 | tf_op jit(solution)/shard_map/ppermute | solution.py:15
  272.0 13.3 %copy-start.1 = (bf16[1792,128]{1,0:T(8,128)(2,1)S(1)}, bf16[1792,128]{1,0:T(8,128)(2,1)}, u32[]{:S(2)}) copy-start(bf16[1792,128]{1,0:T(8,128)(2,1)} %get-tuple-element.8) | copy-start | bytes 1376260
  284.8 72.2 %collective-permute-start.3 = (f32[1792,128]{1,0:T(8,128)}, f32[1792,128]{1,0:T(8,128)}, u32[]{:S(2)}, u32[]{:S(2)}) collective-permute-start(f32[1792,128]{1,0:T(8,128)} %convolution_bitcast_fusion), channel_id=1, source_target_pairs={{0,1},{1,0},{2,3},{3,2},{4,5},{5,4},{6,7},{7,6},{8,9},{9,8},{10,11... | collective-permute-start | bytes 2752520 | tf_op jit(solution)/shard_map/ppermute | solution.py:15
  354.5 2.5 copy-start.3
Sparse Core Ops, SparseCore 0:
  11.7 68.9 all-gather.2
  84.6 68.1 all-reduce.2
  180.4 66.2 all-gather.4
  286.4 68.0 all-reduce.4

commit v2 on v1

--- a/solution.py
+++ b/solution.py
@@ -1,10 +1,16 @@
+import functools
+
 import jax
 import jax.numpy as jnp
 from jax import lax
+from jax.experimental import pallas as pl
+from jax.experimental.pallas import tpu as pltpu
 from jax.sharding import PartitionSpec as P
 
-K = 14336
 BLK = 128
+CHUNK = 2 * BLK
+MESH = pl.DeviceIdType.MESH
+TRANSPOSED = (((0,), (0,)), ((), ()))
 
 
 damping_ratio = 0.3
@@ -82,13 +88,443 @@
     grad_square, grad_curve, curve_square, trace_total = lax.psum(
         jnp.stack([local_square, local_curve, local_curve_square, trace_part]), ("row", "col")
     )
-    damping = damping_ratio * trace_total / K
+    damping = damping_ratio * trace_total / (row_block * lax.axis_size("row"))
     step_first = grad_square / (grad_curve + damping * grad_square + epsilon)
     step_second = (grad_curve + damping * grad_square) / (
         curve_square + 2.0 * damping * grad_curve + damping * damping * grad_square + epsilon
     )
     grad_second = grad_first - step_first * curvature
     return kept_weights - step_first * step_dir - step_second * (mask_local * grad_second)
+
+
+def fused_kernel(
+    n, gram, acts, weights, mask, out,
+    g_vm, xo, xp, y_own, y_oth, y_rx, grad, rs_send, rs_recv, ag_send, ag_recv,
+    trace_row, tot_send, tot_recv,
+    g_sem, ring_ssem, ring_rsem, par_ssem, par_rsem, y_ssem, y_rsem,
+    rs_ssem, rs_rsem, ag_ssem, ag_rsem, tot_ssem, tot_rsem,
+):
+    rows, width = weights.shape
+    nb = gram.shape[1] // rows
+    nz = n // 2
+    chunks = rows // CHUNK
+    split = (chunks + 1) // 2
+    last = n // 2 - 1
+    piece = rs_send.shape[2]
+    blocks = rows // BLK
+    group = lax.axis_index("groups")
+    row = lax.axis_index("row")
+    col = lax.axis_index("col")
+    near_half = row // nb
+
+    def row_of(place):
+        place = lax.rem(place + 2 * n, n)
+        x = place // nz
+        z = place + x * (n - 1 - 2 * place)
+        return 2 * z + x
+
+    my_z, my_x = row // 2, lax.rem(row, 2)
+    place = my_z + my_x * (n - 1 - 2 * my_z)
+    right, left = row_of(place + 1), row_of(place - 1)
+
+    def mask_at(block):
+        return mask[row * blocks + block, col].astype(jnp.float32)
+
+    def ring(phase, way, hop, j):
+        source = row_of(place - hop) if way == 0 else row_of(place + hop)
+        part = xo.at[phase, source, pl.ds(pl.multiple_of(j * CHUNK, CHUNK), CHUNK)]
+        return pltpu.make_async_remote_copy(
+            src_ref=part, dst_ref=part,
+            send_sem=ring_ssem.at[phase, way, hop, j], recv_sem=ring_rsem.at[phase, way, hop, j],
+            device_id=(group, right if way == 0 else left, col), device_id_type=MESH,
+        )
+
+    def ring_arrival(phase, way, hop, j):
+        source = row_of(place - hop - 1) if way == 0 else row_of(place + hop + 1)
+        part = xo.at[phase, source, pl.ds(pl.multiple_of(j * CHUNK, CHUNK), CHUNK)]
+        return pltpu.make_async_remote_copy(
+            src_ref=part, dst_ref=part,
+            send_sem=ring_ssem.at[phase, way, hop, j], recv_sem=ring_rsem.at[phase, way, hop, j],
+            device_id=(group, right if way == 0 else left, col), device_id_type=MESH,
+        )
+
+    def to_partner(phase, source, j):
+        span = pl.ds(pl.multiple_of(j * CHUNK, CHUNK), CHUNK)
+        return pltpu.make_async_remote_copy(
+            src_ref=xo.at[phase, source, span], dst_ref=xp.at[phase, lax.rem(source, nb), span],
+            send_sem=par_ssem.at[phase, lax.rem(source, nb), j],
+            recv_sem=par_rsem.at[phase, lax.rem(source, nb), j],
+            device_id=(group, row, 1 - col), device_id_type=MESH,
+        )
+
+    def y_copy(phase, j):
+        span = pl.ds(pl.multiple_of(j * CHUNK, CHUNK), CHUNK)
+        return pltpu.make_async_remote_copy(
+            src_ref=y_oth.at[phase, span], dst_ref=y_rx.at[phase, span],
+            send_sem=y_ssem.at[phase, j], recv_sem=y_rsem.at[phase, j],
+            device_id=(group, row, 1 - col), device_id_type=MESH,
+        )
+
+    def rs_copy(phase, peer, slot):
+        return pltpu.make_async_remote_copy(
+            src_ref=rs_send.at[phase, peer], dst_ref=rs_recv.at[phase, slot],
+            send_sem=rs_ssem.at[phase, peer], recv_sem=rs_rsem.at[phase, slot],
+            device_id=(group, peer, col), device_id_type=MESH,
+        )
+
+    def ag_copy(phase, peer, slot):
+        return pltpu.make_async_remote_copy(
+            src_ref=ag_send.at[phase], dst_ref=ag_recv.at[phase, slot],
+            send_sem=ag_ssem.at[phase, peer], recv_sem=ag_rsem.at[phase, slot],
+            device_id=(group, peer, col), device_id_type=MESH,
+        )
+
+    me = row * 2 + col
+
+    def tot_copy(peer, slot):
+        return pltpu.make_async_remote_copy(
+            src_ref=tot_send, dst_ref=tot_recv.at[slot],
+            send_sem=tot_ssem.at[peer], recv_sem=tot_rsem.at[slot],
+            device_id=(group, peer // 2, lax.rem(peer, 2)), device_id_type=MESH,
+        )
+
+    def send_own(phase, j):
+        @pl.when(near_half != col)
+        def _():
+            to_partner(phase, row, j).start()
+
+        ring(phase, 0, 0, j).start()
+        ring(phase, 1, 0, j).start()
+
+    def send_inner(phase):
+        inner = jnp.dot(
+            acts[...], xo[phase, row], preferred_element_type=jnp.float32
+        )
+        for peer in range(n):
+            rs_send[phase, peer] = inner[peer * piece:(peer + 1) * piece]
+        for k in range(1, n):
+            rs_copy(phase, lax.rem(row + k, n), row).start()
+
+    def share_inner(phase):
+        total = rs_send[phase, row]
+        for k in range(1, n):
+            peer = lax.rem(row + k, n)
+            rs_copy(phase, peer, peer).wait_recv()
+            total = total + rs_recv[phase, peer]
+        ag_send[phase] = total
+        ag_recv[phase, row] = total
+        for k in range(1, n):
+            ag_copy(phase, lax.rem(row + k, n), row).start()
+
+    def get_inner(phase):
+        for k in range(1, n):
+            peer = lax.rem(row + k, n)
+            ag_copy(phase, peer, peer).wait_recv()
+        inner = ag_recv[phase].reshape(n * piece, width)
+        high = inner.astype(jnp.bfloat16)
+        low = (inner - high.astype(jnp.float32)).astype(jnp.bfloat16)
+        return jnp.concatenate([high, low], axis=1)
+
+    def process(phase, source, j):
+        @pl.when(source // nb != col)
+        def _():
+            @pl.when(source != row)
+            def _():
+                to_partner(phase, source, j).start()
+
+        @pl.when(source // nb == col)
+        def _():
+            to_partner(phase, source, j).wait_recv()
+            span = pl.ds(pl.multiple_of(j * CHUNK, CHUNK), CHUNK)
+            block = lax.rem(source, nb)
+            panel = jnp.concatenate([xo[phase, source, span], xp[phase, block, span]], axis=1)
+
+            @pl.loop(0, 2)
+            def _(tile):
+                at = pl.ds(pl.multiple_of(tile * (rows // 2), rows // 2), rows // 2)
+                got = jnp.dot(
+                    g_vm[block, at, span], panel, preferred_element_type=jnp.float32
+                )
+                y_own[at] += got[:, :width]
+                y_oth[phase, at] += got[:, width:]
+
+    def gather_and_multiply(phase):
+        for hop in range(last):
+            if hop == min(1, last - 1):
+                share_inner(phase)
+
+            @pl.loop(0, chunks)
+            def _(j):
+                for way in range(2):
+                    ring_arrival(phase, way, hop, j).wait_recv()
+                    if hop + 1 < last:
+                        ring(phase, way, hop + 1, j).start()
+                    else:
+                        @pl.when(j < split if way == 0 else j >= split)
+                        def _():
+                            ring(phase, way, hop + 1, j).start()
+                process(phase, row_of(place - hop - 1), j)
+                process(phase, row_of(place + hop + 1), j)
+                if hop == min(1, last - 1):
+                    process(phase, row, j)
+
+        far = row_of(place + n // 2)
+
+        @pl.loop(0, chunks)
+        def _(j):
+            @pl.when(j < split)
+            def _():
+                ring_arrival(phase, 0, last, j).wait_recv()
+
+            @pl.when(j >= split)
+            def _():
+                ring_arrival(phase, 1, last, j).wait_recv()
+
+            @pl.when(far // nb != col)
+            def _():
+                to_partner(phase, far, j).start()
+
+        block = lax.rem(far, nb)
+
+        @pl.when(far // nb == col)
+        def _():
+            @pl.loop(0, chunks)
+            def _(j):
+                to_partner(phase, far, j).wait_recv()
+
+            panel = jnp.concatenate([xo[phase, far], xp[phase, block]], axis=1)
+
+            @pl.loop(0, chunks)
+            def _(j):
+                at = pl.ds(pl.multiple_of(j * CHUNK, CHUNK), CHUNK)
+                got = jnp.dot(g_vm[block, at], panel, preferred_element_type=jnp.float32)
+                y_own[at] += got[:, :width]
+                y_oth[phase, at] += got[:, width:]
+                y_copy(phase, j).start()
+
+        @pl.when(far // nb != col)
+        def _():
+            @pl.loop(0, chunks)
+            def _(j):
+                y_copy(phase, j).start()
+
+    def product(phase, j, inner):
+        y_copy(phase, j).wait_recv()
+        span = pl.ds(pl.multiple_of(j * CHUNK, CHUNK), CHUNK)
+        both = lax.dot_general(
+            acts[:, span], inner, TRANSPOSED, preferred_element_type=jnp.float32
+        )
+        return y_own[span] + y_rx[phase, span] + (both[:, :width] + both[:, width:])
+
+    def fold(values):
+        return jnp.sum(values.reshape(-1, 8, width), axis=0)
+
+    for b in range(nb):
+        pltpu.make_async_copy(
+            gram.at[:, pl.ds(b * rows, rows)], g_vm.at[b], g_sem.at[b]
+        ).start()
+    barrier = pltpu.get_barrier_semaphore()
+    for k in range(1, 2 * n):
+        peer = lax.rem(me + k, 2 * n)
+        pl.semaphore_signal(
+            barrier, inc=1, device_id=(group, peer // 2, lax.rem(peer, 2)), device_id_type=MESH
+        )
+    for i in range(blocks):
+        at = pl.ds(i * BLK, BLK)
+        w = weights[at]
+        xo[0, row, at] = (mask_at(i) * w - w).astype(jnp.bfloat16)
+    y_own[...] = jnp.zeros_like(y_own)
+    y_oth[...] = jnp.zeros_like(y_oth)
+    pl.semaphore_wait(barrier, 2 * n - 1)
+    send_inner(0)
+
+    @pl.loop(0, chunks)
+    def _(j):
+        send_own(0, j)
+
+    for b in range(nb):
+        pltpu.make_async_copy(
+            gram.at[:, pl.ds(b * rows, rows)], g_vm.at[b], g_sem.at[b]
+        ).wait()
+
+    trace_row[...] = jnp.zeros_like(trace_row)
+
+    @pl.when(near_half == col)
+    def _():
+        own = lax.rem(row, nb)
+        eye = lax.broadcasted_iota(jnp.int32, (BLK, BLK), 0) == lax.broadcasted_iota(
+            jnp.int32, (BLK, BLK), 1
+        )
+        total = jnp.zeros((1, BLK), jnp.float32)
+        for i in range(blocks):
+            at = pl.ds(i * BLK, BLK)
+            diagonal = jnp.where(eye, g_vm[own, at, at].astype(jnp.float32), 0.0)
+            act = acts[:, at].astype(jnp.float32)
+            total = total + jnp.sum(diagonal, axis=0, keepdims=True) + jnp.sum(
+                act * act, axis=0, keepdims=True
+            )
+        trace_row[0:1] = total
+
+    gather_and_multiply(0)
+    inner = get_inner(0)
+
+    @pl.loop(0, chunks)
+    def _(j):
+        gradient = product(0, j, inner)
+        span = pl.ds(pl.multiple_of(j * CHUNK, CHUNK), CHUNK)
+        grad[span] = gradient
+        y_own[span] = jnp.zeros_like(gradient)
+        for i in range(CHUNK // BLK):
+            at = pl.ds(pl.multiple_of(j * CHUNK + i * BLK, BLK), BLK)
+            step = mask_at(j * (CHUNK // BLK) + i) * gradient[i * BLK:(i + 1) * BLK]
+            xo[1, row, at] = step.astype(jnp.bfloat16)
+        send_own(1, j)
+
+    send_inner(1)
+    gather_and_multiply(1)
+    inner = get_inner(1)
+
+    def sums(j, carry):
+        square, curve, curve_square = carry
+        curvature = product(1, j, inner)
+        span = pl.ds(pl.multiple_of(j * CHUNK, CHUNK), CHUNK)
+        y_own[span] = curvature
+        for i in range(CHUNK // BLK):
+            at = pl.ds(pl.multiple_of(j * CHUNK + i * BLK, BLK), BLK)
+            keep = mask_at(j * (CHUNK // BLK) + i)
+            step = keep * grad[at]
+            curved = curvature[i * BLK:(i + 1) * BLK]
+            square = square + fold(step * step)
+            curve = curve + fold(step * curved)
+            curve_square = curve_square + fold((keep * curved) * (keep * curved))
+        return square, curve, curve_square
+
+    zero = jnp.zeros((8, width), jnp.float32)
+    parts = lax.fori_loop(0, chunks, sums, (zero, zero, zero))
+    tot_send[...] = jnp.concatenate(
+        [jnp.sum(part, axis=0, keepdims=True) for part in parts] + [trace_row[0:1], zero[:4]], axis=0
+    )
+    tot_recv[me] = tot_send[...]
+    for k in range(1, 2 * n):
+        tot_copy(lax.rem(me + k, 2 * n), me).start()
+    for k in range(1, 2 * n):
+        peer = lax.rem(me + k, 2 * n)
+        tot_copy(peer, peer).wait_recv()
+    totals = jnp.sum(jnp.sum(tot_recv[...], axis=0), axis=1, keepdims=True)
+    grad_square, grad_curve, curve_square, trace_total = (totals[i:i + 1] for i in range(4))
+    damping = damping_ratio * trace_total / (n * rows)
+    step_first = grad_square / (grad_curve + damping * grad_square + epsilon)
+    step_second = (grad_curve + damping * grad_square) / (
+        curve_square + 2.0 * damping * grad_curve + damping * damping * grad_square + epsilon
+    )
+
+    @pl.loop(0, blocks)
+    def _(i):
+        at = pl.ds(pl.multiple_of(i * BLK, BLK), BLK)
+        keep = mask_at(i)
+        gradient = grad[at]
+        second = gradient - step_first * y_own[at]
+        out[at] = keep * weights[at] - step_first * (keep * gradient) - step_second * (keep * second)
+
+    for phase in range(2):
+        @pl.loop(0, chunks)
+        def _(j):
+            for hop in range(last):
+                for way in range(2):
+                    ring(phase, way, hop, j).wait_send()
+
+            @pl.when(j < split)
+            def _():
+                ring(phase, 0, last, j).wait_send()
+
+            @pl.when(j >= split)
+            def _():
+                ring(phase, 1, last, j).wait_send()
+
+            for b in range(nb):
+                to_partner(phase, (1 - col) * nb + b, j).wait_send()
+            y_copy(phase, j).wait_send()
+
+        for k in range(1, n):
+            peer = lax.rem(row + k, n)
+            rs_copy(phase, peer, row).wait_send()
+            ag_copy(phase, peer, row).wait_send()
+    for k in range(1, 2 * n):
+        tot_copy(lax.rem(me + k, 2 * n), me).wait_send()
+
+
+def fused_device(gram_old, activations, weights, block_mask):
+    n = lax.axis_size("row")
+    rows, width = weights.shape
+    depth = activations.shape[0]
+    nb = gram_old.shape[1] // rows
+    chunks = rows // CHUNK
+    hops = n // 2
+    piece = depth // n
+    low, wide = jnp.bfloat16, jnp.float32
+    dma = pltpu.SemaphoreType.DMA
+    return pl.pallas_call(
+        functools.partial(fused_kernel, n),
+        out_shape=jax.ShapeDtypeStruct((rows, width), wide),
+        in_specs=[
+            pl.BlockSpec(memory_space=pl.ANY),
+            pl.BlockSpec(memory_space=pltpu.VMEM),
+            pl.BlockSpec(memory_space=pltpu.VMEM),
+            pl.BlockSpec(memory_space=pltpu.SMEM),
+        ],
+        out_specs=pl.BlockSpec(memory_space=pltpu.VMEM),
+        scratch_shapes=[
+            pltpu.VMEM((nb, rows, rows), low),
+            pltpu.VMEM((2, n, rows, width), low),
+            pltpu.VMEM((2, nb, rows, width), low),
+            pltpu.VMEM((rows, width), wide),
+            pltpu.VMEM((2, rows, width), wide),
+            pltpu.VMEM((2, rows, width), wide),
+            pltpu.VMEM((rows, width), wide),
+            pltpu.VMEM((2, n, piece, width), wide),
+            pltpu.VMEM((2, n, piece, width), wide),
+            pltpu.VMEM((2, piece, width), wide),
+            pltpu.VMEM((2, n, piece, width), wide),
+            pltpu.VMEM((8, width), wide),
+            pltpu.VMEM((8, width), wide),
+            pltpu.VMEM((2 * n, 8, width), wide),
+            dma((nb,)),
+            dma((2, 2, hops, chunks)),
+            dma((2, 2, hops, chunks)),
+            dma((2, nb, chunks)),
+            dma((2, nb, chunks)),
+            dma((2, chunks)),
+            dma((2, chunks)),
+            dma((2, n)),
+            dma((2, n)),
+            dma((2, n)),
+            dma((2, n)),
+            dma((2 * n,)),
+            dma((2 * n,)),
+        ],
+        compiler_params=pltpu.CompilerParams(
+            collective_id=0, has_side_effects=True, vmem_limit_bytes=62 * 1024 * 1024
+        ),
+        name="fused_steps",
+    )(gram_old, activations, weights, block_mask)
+
+
+def fits(gram_old, activations, weights, n):
+    rows, width = weights.shape
+    return (
+        rows % CHUNK == 0
+        and width == BLK
+        and n % 4 == 0
+        and gram_old.shape[1] == rows * n // 2
+        and activations.shape[0] % (8 * n) == 0
+        and gram_old.size <= 14 * 1024 * 1024
+    )
+
+
+def one_device(gram_old, activations, weights, block_mask):
+    if fits(gram_old, activations, weights, lax.axis_size("row")):
+        return fused_device(gram_old, activations, weights, block_mask)
+    return per_device(gram_old, activations, weights, block_mask)
 
 
 def solution(mesh):
@@ -99,7 +535,7 @@
         P(None, "groups"),
     )
     return jax.shard_map(
-        per_device,
+        one_device,
         mesh=mesh,
         in_specs=placed,
         out_specs=P("row", ("groups", "col")),

time: 420 us -> 181 us (0.43)
  waiting for transfers between devices: 270 us -> 0 us
  Pallas kernels: 0 us -> 178 us
  matrix products: 63.5 us -> 0 us
  blocking collectives: 30.3 us -> 0 us
  other arithmetic: 29.6 us -> 0 us
  between operations: 20.8 us -> 0.01 us
    pallas_call x0 -> x1, Pallas kernels: none -> 178 us  [fused_device(): pl.pallas_call(functools.partial(fused_kernel, n), out_shape=jax.ShapeDty...]
    all_gather x2 -> x0, waiting for transfers between devices: 135 us -> none  [apply_gram(): column_panel = lax.all_gather(panel_low, 'row', axis=0, tiled=True)]
    psum x2 -> x0, waiting for transfers between devices: 134 us -> none  [apply_gram(): lax.psum(jnp.dot(activations, panel_low, preferred_element_type=jnp.float...]
    dot_general x12 -> x0, matrix products: 63.5 us -> none  [the longest x2 25.8 us: apply_gram(): own_part = jnp.dot(gram_old, own_half, preferred_element_type=jnp.float32)]
    psum x1 -> x0, blocking collectives: 30.3 us -> none  [per_device(): lax.psum(jnp.stack([local_square, local_curve, local_curve_square, trace_...]
    reduce_sum x2 -> x0, other arithmetic: 24.4 us -> none  [the longest x1 23.6 us: per_device(): jnp.sum(jnp.where(on_diagonal, gram_old.astype(jnp.float32), 0.0))]
    dynamic_slice x2 -> x0, local copies, waits for them, and re-layouts: 4.48 us -> none  [apply_gram(): lax.dynamic_slice_in_dim(column_panel, (1 - col_index) * half_width, half...]
  transfers between devices with their start and end apart: 8 -> 0, of which waited for: 4 -> 0; matrix products, arithmetic and copies ran while one was open for 10% -> 0% of each run, Pallas kernels for 0% -> 0%
where the time goes in v2:
time: 181 us
  Pallas kernels  178 us (98%)
  local copies, waits for them, and re-layouts  3.56 us (2%)
    pallas_call x1, Pallas kernels, fused_device(): pl.pallas_call(functools.partial(fused_kernel, n), out_shape=jax.ShapeDty...  178 us

profile of v2, /device:TPU:0, one launch (start us, length us, event | category | flops | bytes accessed | tf_op | source)
XLA Modules:
  0.0 181.2 jit_solution(5753705263846765908)
XLA Ops:
  0.0 1.4 copy.5.mask
  1.4 177.6 %fused_steps.1 = f32[1792,128]{1,0:T(8,128)} custom-call(bf16[1792,7168]{1,0:T(8,128)(2,1)} %gram.1, bf16[128,1792]{1,0:T(8,128)(2,1)} %acts.1, f32[1792,128]{1,0:T(8,128)} %weights.1, s32[112,2]{1,0:T(8,128)} %copy.5.mask), custom_call_target="tpu_custom_call" | custom-call | tf_op jit(solution)/shard_map/fused_steps/pallas_call | solution.py:466
  179.0 2.2 %copy.7 = f32[1792,128]{1,0:T(8,128)} copy(f32[1792,128]{1,0:T(8,128)} %fused_steps.1) | data formatting | bytes 1835008

commit v3 on v2

--- a/solution.py
+++ b/solution.py
@@ -8,7 +8,7 @@
 from jax.sharding import PartitionSpec as P
 
 BLK = 128
-CHUNK = 2 * BLK
+CUTS = 2
 MESH = pl.DeviceIdType.MESH
 TRANSPOSED = (((0,), (0,)), ((), ()))
 
@@ -99,18 +99,19 @@
 
 def fused_kernel(
     n, gram, acts, weights, mask, out,
-    g_vm, xo, xp, y_own, y_oth, y_rx, grad, rs_send, rs_recv, ag_send, ag_recv,
+    g_vm, xo, xp, y_own, y_oth, y_rx, grad, red_send, red_recv,
     trace_row, tot_send, tot_recv,
     g_sem, ring_ssem, ring_rsem, par_ssem, par_rsem, y_ssem, y_rsem,
-    rs_ssem, rs_rsem, ag_ssem, ag_rsem, tot_ssem, tot_rsem,
+    red_ssem, red_rsem, tot_ssem, tot_rsem,
 ):
     rows, width = weights.shape
     nb = gram.shape[1] // rows
     nz = n // 2
-    chunks = rows // CHUNK
+    chunks = CUTS
+    CHUNK = rows // CUTS
     split = (chunks + 1) // 2
     last = n // 2 - 1
-    piece = rs_send.shape[2]
+    steps = red_send.shape[1]
     blocks = rows // BLK
     group = lax.axis_index("groups")
     row = lax.axis_index("row")
@@ -128,7 +129,7 @@
     right, left = row_of(place + 1), row_of(place - 1)
 
     def mask_at(block):
-        return mask[row * blocks + block, col].astype(jnp.float32)
+        return mask[col, row * blocks + block].astype(jnp.float32)
 
     def ring(phase, way, hop, j):
         source = row_of(place - hop) if way == 0 else row_of(place + hop)
@@ -165,27 +166,29 @@
             device_id=(group, row, 1 - col), device_id_type=MESH,
         )
 
-    def rs_copy(phase, peer, slot):
-        return pltpu.make_async_remote_copy(
-            src_ref=rs_send.at[phase, peer], dst_ref=rs_recv.at[phase, slot],
-            send_sem=rs_ssem.at[phase, peer], recv_sem=rs_rsem.at[phase, slot],
-            device_id=(group, peer, col), device_id_type=MESH,
-        )
-
-    def ag_copy(phase, peer, slot):
-        return pltpu.make_async_remote_copy(
-            src_ref=ag_send.at[phase], dst_ref=ag_recv.at[phase, slot],
-            send_sem=ag_ssem.at[phase, peer], recv_sem=ag_rsem.at[phase, slot],
-            device_id=(group, peer, col), device_id_type=MESH,
+    def across(index, step):
+        return index + (1 - 2 * lax.rem(index // 2 ** step, 2)) * 2 ** step
+
+    def red_copy(phase, step):
+        return pltpu.make_async_remote_copy(
+            src_ref=red_send.at[phase, step], dst_ref=red_recv.at[phase, step],
+            send_sem=red_ssem.at[phase, step], recv_sem=red_rsem.at[phase, step],
+            device_id=(group, across(row, step), col), device_id_type=MESH,
         )
 
     me = row * 2 + col
 
-    def tot_copy(peer, slot):
-        return pltpu.make_async_remote_copy(
-            src_ref=tot_send, dst_ref=tot_recv.at[slot],
-            send_sem=tot_ssem.at[peer], recv_sem=tot_rsem.at[slot],
+    def tot_copy(step):
+        peer = across(me, step)
+        return pltpu.make_async_remote_copy(
+            src_ref=tot_send.at[step], dst_ref=tot_recv.at[step],
+            send_sem=tot_ssem.at[step], recv_sem=tot_rsem.at[step],
             device_id=(group, peer // 2, lax.rem(peer, 2)), device_id_type=MESH,
+        )
+
+    def gram_copy(b):
+        return pltpu.make_async_copy(
+            gram.at[:, pl.ds(pl.multiple_of(b * rows, rows), rows)], g_vm.at[b], g_sem.at[b]
         )
 
     def send_own(phase, j):
@@ -197,101 +200,82 @@
         ring(phase, 1, 0, j).start()
 
     def send_inner(phase):
-        inner = jnp.dot(
+        red_send[phase, 0] = jnp.dot(
             acts[...], xo[phase, row], preferred_element_type=jnp.float32
         )
-        for peer in range(n):
-            rs_send[phase, peer] = inner[peer * piece:(peer + 1) * piece]
-        for k in range(1, n):
-            rs_copy(phase, lax.rem(row + k, n), row).start()
-
-    def share_inner(phase):
-        total = rs_send[phase, row]
-        for k in range(1, n):
-            peer = lax.rem(row + k, n)
-            rs_copy(phase, peer, peer).wait_recv()
-            total = total + rs_recv[phase, peer]
-        ag_send[phase] = total
-        ag_recv[phase, row] = total
-        for k in range(1, n):
-            ag_copy(phase, lax.rem(row + k, n), row).start()
-
-    def get_inner(phase):
-        for k in range(1, n):
-            peer = lax.rem(row + k, n)
-            ag_copy(phase, peer, peer).wait_recv()
-        inner = ag_recv[phase].reshape(n * piece, width)
+        red_copy(phase, 0).start()
+
+    def reduce_inner(phase, step):
+        red_copy(phase, step).wait_recv()
+        return red_send[phase, step] + red_recv[phase, step]
+
+    def add_update(phase):
+        inner = reduce_inner(phase, steps - 1)
         high = inner.astype(jnp.bfloat16)
         low = (inner - high.astype(jnp.float32)).astype(jnp.bfloat16)
-        return jnp.concatenate([high, low], axis=1)
-
-    def process(phase, source, j):
+        pair = jnp.concatenate([high, low], axis=1)
+
+        @pl.loop(0, blocks)
+        def _(i):
+            at = pl.ds(pl.multiple_of(i * BLK, BLK), BLK)
+            both = lax.dot_general(
+                acts[:, at], pair, TRANSPOSED, preferred_element_type=jnp.float32
+            )
+            y_own[at] += both[:, :width] + both[:, width:]
+
+    def process(phase, source):
+        @pl.when(source // nb == col)
+        def _():
+            for j in range(chunks):
+                to_partner(phase, source, j).wait_recv()
+            block = lax.rem(source, nb)
+            panel = jnp.concatenate([xo[phase, source], xp[phase, block]], axis=1)
+
+            @pl.loop(0, chunks)
+            def _(tile):
+                at = pl.ds(pl.multiple_of(tile * CHUNK, CHUNK), CHUNK)
+                got = jnp.dot(g_vm[block, at], panel, preferred_element_type=jnp.float32)
+                y_own[at] += got[:, :width]
+                y_oth[phase, at] += got[:, width:]
+
+    def relay(phase, source, j):
         @pl.when(source // nb != col)
         def _():
-            @pl.when(source != row)
-            def _():
-                to_partner(phase, source, j).start()
-
-        @pl.when(source // nb == col)
-        def _():
-            to_partner(phase, source, j).wait_recv()
-            span = pl.ds(pl.multiple_of(j * CHUNK, CHUNK), CHUNK)
-            block = lax.rem(source, nb)
-            panel = jnp.concatenate([xo[phase, source, span], xp[phase, block, span]], axis=1)
-
-            @pl.loop(0, 2)
-            def _(tile):
-                at = pl.ds(pl.multiple_of(tile * (rows // 2), rows // 2), rows // 2)
-                got = jnp.dot(
-                    g_vm[block, at, span], panel, preferred_element_type=jnp.float32
-                )
-                y_own[at] += got[:, :width]
-                y_oth[phase, at] += got[:, width:]
+            to_partner(phase, source, j).start()
 
     def gather_and_multiply(phase):
+        if phase == 0:
+            gram_copy(lax.rem(row, nb)).wait()
+        process(phase, row)
+        if phase == 0:
+            for b in range(1, nb):
+                gram_copy(lax.rem(row + b, nb)).wait()
         for hop in range(last):
-            if hop == min(1, last - 1):
-                share_inner(phase)
-
-            @pl.loop(0, chunks)
-            def _(j):
+            for j in range(chunks):
                 for way in range(2):
                     ring_arrival(phase, way, hop, j).wait_recv()
-                    if hop + 1 < last:
+                    if hop + 1 < last or (j < split) == (way == 0):
                         ring(phase, way, hop + 1, j).start()
-                    else:
-                        @pl.when(j < split if way == 0 else j >= split)
-                        def _():
-                            ring(phase, way, hop + 1, j).start()
-                process(phase, row_of(place - hop - 1), j)
-                process(phase, row_of(place + hop + 1), j)
-                if hop == min(1, last - 1):
-                    process(phase, row, j)
+                    relay(phase, row_of(place + (2 * way - 1) * (hop + 1)), j)
+            if hop < steps - 1:
+                red_send[phase, hop + 1] = reduce_inner(phase, hop)
+                red_copy(phase, hop + 1).start()
+
+            @pl.loop(0, 2)
+            def _(way):
+                process(phase, row_of(place + (2 * way - 1) * (hop + 1)))
+        add_update(phase)
 
         far = row_of(place + n // 2)
-
-        @pl.loop(0, chunks)
-        def _(j):
-            @pl.when(j < split)
-            def _():
-                ring_arrival(phase, 0, last, j).wait_recv()
-
-            @pl.when(j >= split)
-            def _():
-                ring_arrival(phase, 1, last, j).wait_recv()
-
-            @pl.when(far // nb != col)
-            def _():
-                to_partner(phase, far, j).start()
-
+        for j in range(chunks):
+            ring_arrival(phase, 0 if j < split else 1, last, j).wait_recv()
+            relay(phase, far, j)
         block = lax.rem(far, nb)
 
         @pl.when(far // nb == col)
         def _():
-            @pl.loop(0, chunks)
-            def _(j):
+            for j in range(chunks):
                 to_partner(phase, far, j).wait_recv()
-
             panel = jnp.concatenate([xo[phase, far], xp[phase, block]], axis=1)
 
             @pl.loop(0, chunks)
@@ -304,49 +288,45 @@
 
         @pl.when(far // nb != col)
         def _():
-            @pl.loop(0, chunks)
-            def _(j):
+            for j in range(chunks):
                 y_copy(phase, j).start()
-
-    def product(phase, j, inner):
-        y_copy(phase, j).wait_recv()
-        span = pl.ds(pl.multiple_of(j * CHUNK, CHUNK), CHUNK)
-        both = lax.dot_general(
-            acts[:, span], inner, TRANSPOSED, preferred_element_type=jnp.float32
-        )
-        return y_own[span] + y_rx[phase, span] + (both[:, :width] + both[:, width:])
 
     def fold(values):
         return jnp.sum(values.reshape(-1, 8, width), axis=0)
 
     for b in range(nb):
-        pltpu.make_async_copy(
-            gram.at[:, pl.ds(b * rows, rows)], g_vm.at[b], g_sem.at[b]
-        ).start()
+        gram_copy(lax.rem(row + b, nb)).start()
     barrier = pltpu.get_barrier_semaphore()
-    for k in range(1, 2 * n):
-        peer = lax.rem(me + k, 2 * n)
-        pl.semaphore_signal(
-            barrier, inc=1, device_id=(group, peer // 2, lax.rem(peer, 2)), device_id_type=MESH
-        )
+    friends = [(right, col), (left, col), (row, 1 - col)]
+    friends += [(across(row, step), col) for step in range(steps)]
+    for friend in friends:
+        pl.semaphore_signal(barrier, inc=1, device_id=(group, *friend), device_id_type=MESH)
     for i in range(blocks):
         at = pl.ds(i * BLK, BLK)
         w = weights[at]
         xo[0, row, at] = (mask_at(i) * w - w).astype(jnp.bfloat16)
     y_own[...] = jnp.zeros_like(y_own)
     y_oth[...] = jnp.zeros_like(y_oth)
-    pl.semaphore_wait(barrier, 2 * n - 1)
+    pl.semaphore_wait(barrier, len(friends))
     send_inner(0)
-
-    @pl.loop(0, chunks)
-    def _(j):
+    for j in range(chunks):
         send_own(0, j)
-
-    for b in range(nb):
-        pltpu.make_async_copy(
-            gram.at[:, pl.ds(b * rows, rows)], g_vm.at[b], g_sem.at[b]
-        ).wait()
-
+    gather_and_multiply(0)
+
+    per_chunk = CHUNK // BLK
+    for j in range(chunks):
+        y_copy(0, j).wait_recv()
+
+        @pl.loop(j * per_chunk, (j + 1) * per_chunk)
+        def _(i):
+            at = pl.ds(pl.multiple_of(i * BLK, BLK), BLK)
+            gradient = y_own[at] + y_rx[0, at]
+            grad[at] = gradient
+            y_own[at] = jnp.zeros_like(gradient)
+            xo[1, row, at] = (mask_at(i) * gradient).astype(jnp.bfloat16)
+
+        send_own(1, j)
+    send_inner(1)
     trace_row[...] = jnp.zeros_like(trace_row)
 
     @pl.when(near_half == col)
@@ -365,52 +345,34 @@
             )
         trace_row[0:1] = total
 
-    gather_and_multiply(0)
-    inner = get_inner(0)
-
-    @pl.loop(0, chunks)
-    def _(j):
-        gradient = product(0, j, inner)
-        span = pl.ds(pl.multiple_of(j * CHUNK, CHUNK), CHUNK)
-        grad[span] = gradient
-        y_own[span] = jnp.zeros_like(gradient)
-        for i in range(CHUNK // BLK):
-            at = pl.ds(pl.multiple_of(j * CHUNK + i * BLK, BLK), BLK)
-            step = mask_at(j * (CHUNK // BLK) + i) * gradient[i * BLK:(i + 1) * BLK]
-            xo[1, row, at] = step.astype(jnp.bfloat16)
-        send_own(1, j)
-
-    send_inner(1)
     gather_and_multiply(1)
-    inner = get_inner(1)
-
-    def sums(j, carry):
+
+    def sums(i, carry):
         square, curve, curve_square = carry
-        curvature = product(1, j, inner)
-        span = pl.ds(pl.multiple_of(j * CHUNK, CHUNK), CHUNK)
-        y_own[span] = curvature
-        for i in range(CHUNK // BLK):
-            at = pl.ds(pl.multiple_of(j * CHUNK + i * BLK, BLK), BLK)
-            keep = mask_at(j * (CHUNK // BLK) + i)
-            step = keep * grad[at]
-            curved = curvature[i * BLK:(i + 1) * BLK]
-            square = square + fold(step * step)
-            curve = curve + fold(step * curved)
-            curve_square = curve_square + fold((keep * curved) * (keep * curved))
+        at = pl.ds(pl.multiple_of(i * BLK, BLK), BLK)
+        curvature = y_own[at] + y_rx[1, at]
+        y_own[at] = curvature
+        keep = mask_at(i)
+        step = keep * grad[at]
+        square = square + fold(step * step)
+        curve = curve + fold(step * curvature)
+        curve_square = curve_square + fold((keep * curvature) * (keep * curvature))
         return square, curve, curve_square
 
     zero = jnp.zeros((8, width), jnp.float32)
-    parts = lax.fori_loop(0, chunks, sums, (zero, zero, zero))
-    tot_send[...] = jnp.concatenate(
+    parts = (zero, zero, zero)
+    for j in range(chunks):
+        y_copy(1, j).wait_recv()
+        parts = lax.fori_loop(j * per_chunk, (j + 1) * per_chunk, sums, parts)
+    total = jnp.concatenate(
         [jnp.sum(part, axis=0, keepdims=True) for part in parts] + [trace_row[0:1], zero[:4]], axis=0
     )
-    tot_recv[me] = tot_send[...]
-    for k in range(1, 2 * n):
-        tot_copy(lax.rem(me + k, 2 * n), me).start()
-    for k in range(1, 2 * n):
-        peer = lax.rem(me + k, 2 * n)
-        tot_copy(peer, peer).wait_recv()
-    totals = jnp.sum(jnp.sum(tot_recv[...], axis=0), axis=1, keepdims=True)
+    for step in range(steps + 1):
+        tot_send[step] = total
+        tot_copy(step).start()
+        tot_copy(step).wait_recv()
+        total = total + tot_recv[step]
+    totals = jnp.sum(total, axis=1, keepdims=True)
     grad_square, grad_curve, curve_square, trace_total = (totals[i:i + 1] for i in range(4))
     damping = damping_ratio * trace_total / (n * rows)
     step_first = grad_square / (grad_curve + damping * grad_square + epsilon)
@@ -427,30 +389,18 @@
         out[at] = keep * weights[at] - step_first * (keep * gradient) - step_second * (keep * second)
 
     for phase in range(2):
-        @pl.loop(0, chunks)
-        def _(j):
+        for j in range(chunks):
             for hop in range(last):
                 for way in range(2):
                     ring(phase, way, hop, j).wait_send()
-
-            @pl.when(j < split)
-            def _():
-                ring(phase, 0, last, j).wait_send()
-
-            @pl.when(j >= split)
-            def _():
-                ring(phase, 1, last, j).wait_send()
-
+            ring(phase, 0 if j < split else 1, last, j).wait_send()
             for b in range(nb):
                 to_partner(phase, (1 - col) * nb + b, j).wait_send()
             y_copy(phase, j).wait_send()
-
-        for k in range(1, n):
-            peer = lax.rem(row + k, n)
-            rs_copy(phase, peer, row).wait_send()
-            ag_copy(phase, peer, row).wait_send()
-    for k in range(1, 2 * n):
-        tot_copy(lax.rem(me + k, 2 * n), me).wait_send()
+        for step in range(steps):
+            red_copy(phase, step).wait_send()
+    for step in range(steps + 1):
+        tot_copy(step).wait_send()
 
 
 def fused_device(gram_old, activations, weights, block_mask):
@@ -458,9 +408,9 @@
     rows, width = weights.shape
     depth = activations.shape[0]
     nb = gram_old.shape[1] // rows
-    chunks = rows // CHUNK
+    chunks = CUTS
     hops = n // 2
-    piece = depth // n
+    steps = n.bit_length() - 1
     low, wide = jnp.bfloat16, jnp.float32
     dma = pltpu.SemaphoreType.DMA
     return pl.pallas_call(
@@ -481,13 +431,11 @@
             pltpu.VMEM((2, rows, width), wide),
             pltpu.VMEM((2, rows, width), wide),
             pltpu.VMEM((rows, width), wide),
-            pltpu.VMEM((2, n, piece, width), wide),
-            pltpu.VMEM((2, n, piece, width), wide),
-            pltpu.VMEM((2, piece, width), wide),
-            pltpu.VMEM((2, n, piece, width), wide),
+            pltpu.VMEM((2, steps, depth, width), wide),
+            pltpu.VMEM((2, steps, depth, width), wide),
             pltpu.VMEM((8, width), wide),
-            pltpu.VMEM((8, width), wide),
-            pltpu.VMEM((2 * n, 8, width), wide),
+            pltpu.VMEM((steps + 1, 8, width), wide),
+            pltpu.VMEM((steps + 1, 8, width), wide),
             dma((nb,)),
             dma((2, 2, hops, chunks)),
             dma((2, 2, hops, chunks)),
@@ -495,28 +443,27 @@
             dma((2, nb, chunks)),
             dma((2, chunks)),
             dma((2, chunks)),
-            dma((2, n)),
-            dma((2, n)),
-            dma((2, n)),
-            dma((2, n)),
-            dma((2 * n,)),
-            dma((2 * n,)),
+            dma((2, steps)),
+            dma((2, steps)),
+            dma((steps + 1,)),
+            dma((steps + 1,)),
         ],
         compiler_params=pltpu.CompilerParams(
             collective_id=0, has_side_effects=True, vmem_limit_bytes=62 * 1024 * 1024
         ),
         name="fused_steps",
-    )(gram_old, activations, weights, block_mask)
+    )(gram_old, activations, weights, block_mask.T)
 
 
 def fits(gram_old, activations, weights, n):
     rows, width = weights.shape
     return (
-        rows % CHUNK == 0
+        rows % (CUTS * BLK) == 0
         and width == BLK
-        and n % 4 == 0
+        and n >= 4
+        and n & (n - 1) == 0
         and gram_old.shape[1] == rows * n // 2
-        and activations.shape[0] % (8 * n) == 0
+        and activations.shape[0] % BLK == 0
         and gram_old.size <= 14 * 1024 * 1024
     )
 

time: 181 us -> 109 us (0.60)
  Pallas kernels: 178 us -> 107 us
    pallas_call x1, Pallas kernels: 178 us -> 107 us  [fused_device(): pl.pallas_call(functools.partial(fused_kernel, n), out_shape=jax.ShapeDty...]
where the time goes in v3:
time: 109 us
  Pallas kernels  107 us (98%)
  local copies, waits for them, and re-layouts  2.16 us (2%)
    pallas_call x1, Pallas kernels, fused_device(): pl.pallas_call(functools.partial(fused_kernel, n), out_shape=jax.ShapeDty...  107 us

profile of v3, /device:TPU:0, one launch (start us, length us, event | category | flops | bytes accessed | tf_op | source)
XLA Modules:
  0.0 109.3 jit_solution(1969870729309615997)
XLA Ops:
  0.0 107.1 %fused_steps.1 = f32[1792,128]{1,0:T(8,128)} custom-call(bf16[1792,7168]{1,0:T(8,128)(2,1)} %gram.1, bf16[128,1792]{1,0:T(8,128)(2,1)} %acts.1, f32[1792,128]{1,0:T(8,128)} %weights.1, s32[2,112]{1,0:T(2,128)} %bitcast.1), custom_call_target="tpu_custom_call" | custom-call | tf_op jit(solution)/shard_map/fused_steps/pallas_call | solution.py:416
  107.1 2.2 %copy.6 = f32[1792,128]{1,0:T(8,128)} copy(f32[1792,128]{1,0:T(8,128)} %fused_steps.1) | data formatting | bytes 1835008

commit v4 on v3

--- a/solution.py
+++ b/solution.py
@@ -308,9 +308,9 @@
     y_own[...] = jnp.zeros_like(y_own)
     y_oth[...] = jnp.zeros_like(y_oth)
     pl.semaphore_wait(barrier, len(friends))
-    send_inner(0)
     for j in range(chunks):
         send_own(0, j)
+    send_inner(0)
     gather_and_multiply(0)
 
     per_chunk = CHUNK // BLK

time: 109 us -> 109 us (level)
  no operation moved by 1% of the time
where the time goes in v4:
time: 109 us
  Pallas kernels  107 us (98%)
  local copies, waits for them, and re-layouts  2.16 us (2%)
    pallas_call x1, Pallas kernels, fused_device(): pl.pallas_call(functools.partial(fused_kernel, n), out_shape=jax.ShapeDty...  107 us

profile of v4, /device:TPU:0, one launch (start us, length us, event | category | flops | bytes accessed | tf_op | source)
XLA Modules:
  0.0 109.0 jit_solution(2970170697938328885)
XLA Ops:
  0.0 106.8 %fused_steps.1 = f32[1792,128]{1,0:T(8,128)} custom-call(bf16[1792,7168]{1,0:T(8,128)(2,1)} %gram.1, bf16[128,1792]{1,0:T(8,128)(2,1)} %acts.1, f32[1792,128]{1,0:T(8,128)} %weights.1, s32[2,112]{1,0:T(2,128)} %bitcast.1), custom_call_target="tpu_custom_call" | custom-call | tf_op jit(solution)/shard_map/fused_steps/pallas_call | solution.py:416
  106.8 2.2 %copy.6 = f32[1792,128]{1,0:T(8,128)} copy(f32[1792,128]{1,0:T(8,128)} %fused_steps.1) | data formatting | bytes 1835008
